TPU v7x, 256 devices: a whole 4x4x8 slice. The times are simulated.
256 devices in a mesh: section: 16 (over x, y_lo, core), dp: 8 (over z), tensor: 2 (over y_hi).
Axes of the slice: x: 4, y: 4 (y_hi: 2, y_lo: 2; y = y_hi * 2 + y_lo), z: 8, core: 2. Of those that a mesh axis runs over, the one named last changes fastest.
Arguments:
- activations: bfloat16 [16, 8192, 2048], P('section', 'dp', 'tensor'), may hold values from -150 to 150, as said below
- sent_grads: bfloat16 [16, 8192, 2048], P('section', 'dp', 'tensor'), may hold values from -150 to 150, as said below
- damping: float32 [16, 2, 2], P('section', None, 'tensor'), may hold values from 0.05 to 0.5
- bubble_steps: int32 [16, 2, 2], P('section', None, 'tensor'), may hold values from 1 to 3
- warm: float32 [16, 2, 2, 1024, 1024], P('section', None, 'tensor', 'dp'), may hold values from -0.02 to 1.2, as said below
Outputs:
- inverse: float32 [16, 2, 2, 1024, 1024], P('section', None, 'tensor', 'dp')
Inputs may be any that keep to these rules, and one draw needn't show every extreme that they name: `activations`: input features of one section's layer, rows and columns of differing scales. `sent_grads`: gradients of one section's layer outputs, rows and columns of differing scales. `warm`: symmetric with a positive diagonal; Newton-Schulz steps from it contract toward the inverse of each block's factor.
All inputs are finite; a program needn't handle non-finite values.
Results may differ from a plain program's by a relative error of at most 0.0003.
Values may be sent and summed in bfloat16 or wider, within the bound.
A program may use at most 192 MiB of HBM per device.

v0:
```python
import jax
import jax.numpy as jnp
from jax import lax
from jax.sharding import PartitionSpec as P

ITERS = 3


def from_behind(value, axis, steps):
    count = lax.axis_size(axis)
    leading, last = (max(0, -steps), min(count, count - steps))
    return lax.ppermute(value, axis, [(source, source + steps) for source in range(leading, last)])


def gram(rows):
    return lax.dot_general(rows, rows, (((0,), (0,)), ((), ())), preferred_element_type=jnp.float32)


def fetch_grads(sent_grads):
    return from_behind(sent_grads, "section", -1)


def newton_step(iterates, factors, counts, index):
    products = tuple(
        (jnp.dot(x, f, precision=lax.Precision.HIGHEST) for x, f in zip(iterates, factors))
    )
    pieces = jax.tree.map(lambda part: lax.all_gather(part, "dp", axis=0, tiled=True), iterates)
    folded = tuple(
        (
            jnp.dot(product, piece, precision=lax.Precision.HIGHEST)
            for product, piece in zip(products, pieces)
        )
    )
    return tuple(
        (jnp.where(index < count, 2.0 * x - t, x) for x, t, count in zip(iterates, folded, counts))
    )


def local(activations, sent_grads, damping, bubble_steps, warm):
    inputs = activations[0]
    received = fetch_grads(sent_grads)
    first_part = gram(inputs)
    second_part = gram(received[0])
    first_sum, second_sum = lax.psum((first_part, second_part), "dp")
    total_tokens = inputs.shape[0] * lax.axis_size("dp")
    identity = jnp.eye(first_sum.shape[0], dtype=jnp.float32)
    factors = (
        first_sum / total_tokens + damping[0, 0, 0] * identity,
        second_sum / total_tokens + damping[0, 1, 0] * identity,
    )
    counts = (bubble_steps[0, 0, 0], bubble_steps[0, 1, 0])
    iterates = (warm[0, 0, 0], warm[0, 1, 0])
    for index in range(ITERS):
        iterates = newton_step(iterates, factors, counts, index)
    return jnp.stack(iterates)[None, :, None]


def solution(mesh):
    placed = (
        P("section", "dp", "tensor"),
        P("section", "dp", "tensor"),
        P("section", None, "tensor"),
        P("section", None, "tensor"),
        P("section", None, "tensor", "dp", None),
    )
    return jax.shard_map(
        local,
        mesh=mesh,
        in_specs=placed,
        out_specs=P("section", None, "tensor", "dp", None),
        check_vma=False,
    )
```

profile of v0, /device:TPU:1, one launch (start us, length us, event | category | flops | bytes accessed | tf_op | source)
XLA Modules:
  0.0 574.6 jit_solution(16592266944513606604)
XLA Ops:
  6.5 5.2 collective-permute-start
  11.8 4.4 fusion.12
  16.2 19.0 %collective-permute-done = bf16[1,1024,1024]{2,1,0:T(8,128)(2,1)S(1)} collective-permute-done((bf16[1,1024,1024]{2,1,0:T(8,128)(2,1)}, bf16[1,1024,1024]{2,1,0:T(8,128)(2,1)S(1)}, u32[]{:S(2)}, u32[]{:S(2)}) %collective-permute-start) | collective-permute-done | bytes 2097184 | tf_op jit(solution)/shard_map/ppermute | solution.py:12
  35.2 4.4 fusion.10
  39.6 1.1 copy-done.5
  44.9 185.7 %all-reduce.3.cloned.1.call-done = (f32[1024,1024]{1,0:T(8,128)}, f32[1024,1024]{1,0:T(8,128)}) async-done(((f32[1024,1024]{1,0:T(8,128)}, f32[1024,1024]{1,0:T(8,128)}), (f32[1024,1024]{1,0:T(8,128)}, f32[1024,1024]{1,0:T(8,128)})) %all-reduce.3.cloned.1.call-update) | async-done | bytes 8388624 | tf_op jit(solution)/shard_map/psum | solution.py:44
  230.6 10.3 %fusion.6 = f32[1024,128]{1,0:T(8,128)} fusion(f32[1024,1024]{1,0:T(8,128)} %get-tuple-element.6, f32[]{:T(128)} %bitcast.5, f32[1,2,1,128,1024]{4,3,2,1,0:T(8,128)S(1)} %copy-done.5), kind=kOutput, calls=%fused_computation.9 | convolution fusion | flops 1614807040 | bytes 5242884 | tf_op jit(solution)/shard_map/dot_general | solution.py:25
  240.9 45.1 %all-gather.17.cloned.1.call-done = f32[1,1,1,1024,1024]{4,3,2,1,0:T(8,128)} async-done(((f32[1,1,1,128,1024]{4,3,2,1,0:T(8,128)}), f32[1,1,1,1024,1024]{4,3,2,1,0:T(8,128)}) %all-gather.17.cloned.1.call-update) | async-done | bytes 4194320 | tf_op jit(solution)/shard_map/all_gather | solution.py:27
  285.9 5.5 fusion.35
  292.3 10.3 %fusion.9 = f32[1024,128]{1,0:T(8,128)} fusion(f32[1024,1024]{1,0:T(8,128)} %get-tuple-element.5, f32[]{:T(128)} %bitcast.13, f32[1,2,1,128,1024]{4,3,2,1,0:T(8,128)S(1)} %copy-done.5), kind=kOutput, calls=%fused_computation.12 | convolution fusion | flops 1614807040 | bytes 5242884 | tf_op jit(solution)/shard_map/dot_general | solution.py:25
  302.6 38.5 %all-gather.19.cloned.1.call-done = f32[1,1,1,1024,1024]{4,3,2,1,0:T(8,128)} async-done(((f32[1,1,1,128,1024]{4,3,2,1,0:T(8,128)}), f32[1,1,1,1024,1024]{4,3,2,1,0:T(8,128)}) %all-gather.19.cloned.1.call-update) | async-done | bytes 4194320 | tf_op jit(solution)/shard_map/all_gather | solution.py:27
  341.1 5.6 fusion.41
  347.4 6.2 %fusion.5 = f32[128,1024]{1,0:T(8,128)} fusion(f32[128,1024]{1,0:T(8,128)S(1)} %copy-done.2, f32[1024,1024]{1,0:T(8,128)} %get-tuple-element.6, f32[]{:T(128)} %bitcast.5), kind=kOutput, calls=%fused_computation.8 | convolution fusion | flops 1614807040 | bytes 5242884 | tf_op jit(solution)/shard_map/dot_general | solution.py:25
  353.6 42.6 %all-gather.9.cloned.1.call-done = f32[1024,1024]{1,0:T(8,128)} async-done(((f32[128,1024]{1,0:T(8,128)}), f32[1024,1024]{1,0:T(8,128)}) %all-gather.9.cloned.1.call-update) | async-done | bytes 4194320 | tf_op jit(solution)/shard_map/all_gather | solution.py:27
  396.2 5.6 fusion.49
  402.6 6.2 %fusion.8 = f32[128,1024]{1,0:T(8,128)} fusion(f32[128,1024]{1,0:T(8,128)S(1)} %copy-done.3, f32[1024,1024]{1,0:T(8,128)} %get-tuple-element.5, f32[]{:T(128)} %bitcast.13), kind=kOutput, calls=%fused_computation.11 | convolution fusion | flops 1614807040 | bytes 5242884 | tf_op jit(solution)/shard_map/dot_general | solution.py:25
  408.8 42.4 %all-gather.13.cloned.1.call-done = f32[1024,1024]{1,0:T(8,128)} async-done(((f32[128,1024]{1,0:T(8,128)}), f32[1024,1024]{1,0:T(8,128)}) %all-gather.13.cloned.1.call-update) | async-done | bytes 4194320 | tf_op jit(solution)/shard_map/all_gather | solution.py:27
  451.2 5.6 fusion.46
  458.4 6.2 %fusion.4 = f32[128,1024]{1,0:T(8,128)} fusion(f32[128,1024]{1,0:T(8,128)S(1)} %copy-done.1, f32[1024,1024]{1,0:T(8,128)} %get-tuple-element.6, f32[]{:T(128)} %bitcast.5), kind=kOutput, calls=%fused_computation.7 | convolution fusion | flops 1614807040 | bytes 5242884 | tf_op jit(solution)/shard_map/dot_general | solution.py:25
  464.6 4.0 fusion.7
  468.6 37.6 %all-gather.11.cloned.1.call-done = f32[1024,1024]{1,0:T(8,128)} async-done(((f32[128,1024]{1,0:T(8,128)}), f32[1024,1024]{1,0:T(8,128)}) %all-gather.11.cloned.1.call-update) | async-done | bytes 4194320 | tf_op jit(solution)/shard_map/all_gather | solution.py:27
  506.2 5.6 fusion.48
  511.8 49.6 %all-gather.15.cloned.1.call-done = f32[1024,1024]{1,0:T(8,128)} async-done(((f32[128,1024]{1,0:T(8,128)}), f32[1024,1024]{1,0:T(8,128)}) %all-gather.15.cloned.1.call-update) | async-done | bytes 4194320 | tf_op jit(solution)/shard_map/all_gather | solution.py:27
  561.6 4.8 fusion.45
  (37 shorter events, 5.2 us)
Async XLA Ops:
  6.5 5.2 copy-start
  6.5 224.1 %all-reduce.3.cloned.1.call-start = ((), (), s32[]{:S(2)}) async-start(), calls=%async_computation.6 | async-start | bytes 16777216 | tf_op jit(solution)/shard_map/psum | solution.py:44
  6.5 28.6 %collective-permute-start = (bf16[1,1024,1024]{2,1,0:T(8,128)(2,1)}, bf16[1,1024,1024]{2,1,0:T(8,128)(2,1)S(1)}, u32[]{:S(2)}, u32[]{:S(2)}) collective-permute-start(bf16[1,1024,1024]{2,1,0:T(8,128)(2,1)} %param.6), channel_id=1, source_target_pairs={{16,0},{32,16},{48,32},{64,48},{80,64},{96,80},{112,96},{128,112},... | collective-permute-start | bytes 6291464 | tf_op jit(solution)/shard_map/ppermute | solution.py:12
  39.5 1.2 copy-start.5
  39.5 3.6 copy-start.7
  39.5 4.7 copy-start.8
  39.6 246.4 %all-gather.17.cloned.1.call-start = ((), (), s32[]{:S(2)}) async-start(), calls=%async_computation.4 | async-start | bytes 4718592 | tf_op jit(solution)/shard_map/all_gather | solution.py:27
  41.8 299.3 %all-gather.19.cloned.1.call-start = ((), (), s32[]{:S(2)}) async-start(), calls=%async_computation.5 | async-start | bytes 4718592 | tf_op jit(solution)/shard_map/all_gather | solution.py:27
  42.6 353.6 %all-gather.9.cloned.1.call-start = ((), (), s32[]{:S(2)}) async-start(), calls=%async_computation | async-start | bytes 4718592 | tf_op jit(solution)/shard_map/all_gather | solution.py:27
  291.5 159.7 %all-gather.13.cloned.1.call-start = ((), (), s32[]{:S(2)}) async-start(), calls=%async_computation.2 | async-start | bytes 4718592 | tf_op jit(solution)/shard_map/all_gather | solution.py:27
  302.6 44.8 %copy-start.2 = (f32[128,1024]{1,0:T(8,128)S(1)}, f32[128,1024]{1,0:T(8,128)}, u32[]{:S(2)}) copy-start(f32[128,1024]{1,0:T(8,128)} %fusion.35) | copy-start | bytes 1572868
  346.8 159.4 %all-gather.11.cloned.1.call-start = ((), (), s32[]{:S(2)}) async-start(), calls=%async_computation.1 | async-start | bytes 4718592 | tf_op jit(solution)/shard_map/all_gather | solution.py:27
  353.6 49.0 %copy-start.3 = (f32[128,1024]{1,0:T(8,128)S(1)}, f32[128,1024]{1,0:T(8,128)}, u32[]{:S(2)}) copy-start(f32[128,1024]{1,0:T(8,128)} %fusion.41) | copy-start | bytes 1572868
  401.8 159.6 %all-gather.15.cloned.1.call-start = ((), (), s32[]{:S(2)}) async-start(), calls=%async_computation.3 | async-start | bytes 4718592 | tf_op jit(solution)/shard_map/all_gather | solution.py:27
  408.8 49.6 %copy-start.1 = (f32[128,1024]{1,0:T(8,128)S(1)}, f32[128,1024]{1,0:T(8,128)}, u32[]{:S(2)}) copy-start(f32[128,1024]{1,0:T(8,128)} %fusion.49) | copy-start | bytes 1572868
  456.7 7.9 %copy-start.4 = (f32[128,1024]{1,0:T(8,128)S(1)}, f32[128,1024]{1,0:T(8,128)}, u32[]{:S(2)}) copy-start(f32[128,1024]{1,0:T(8,128)} %fusion.46) | copy-start | bytes 1572868
  456.8 7.8 %copy-start.9 = (f32[1024,1024]{1,0:T(8,128)S(1)}, f32[1024,1024]{1,0:T(8,128)}, u32[]{:S(2)}) copy-start(f32[1024,1024]{1,0:T(8,128)} %get-tuple-element.5) | copy-start | bytes 12582916
  511.8 54.6 %copy-start.6 = (f32[1,128,1024]{2,1,0:T(8,128)S(1)}, f32[1,128,1024]{2,1,0:T(8,128)}, u32[]{:S(2)}) copy-start(f32[1,128,1024]{2,1,0:T(8,128)} %fusion.48) | copy-start | bytes 1572868
Sparse Core Ops, SparseCore 0:
  39.7 190.8 all-reduce.2
  232.4 53.4 all-gather.16
  287.7 53.3 all-gather.18
  342.8 53.3 all-gather.8
  397.8 53.3 all-gather.12
  452.8 53.3 all-gather.10
  508.0 53.3 all-gather.14
where the time goes:
time: 579 us; the launch traced here: 575 us
  waiting for transfers between devices  461 us (80%)
  matrix products  84.6 us (15%)
  between operations  17.9 us (3%)
  starting transfers between devices  6.39 us (1%)
    all_gather x6, waiting for transfers between devices, newton_step(): lax.all_gather(part, 'dp', axis=0, tiled=True)  256 us
    psum x1, waiting for transfers between devices, local(): first_sum, second_sum = lax.psum((first_part, second_part), 'dp')  186 us
    dot_general x6, matrix products, newton_step(): jnp.dot(x, f, precision=lax.Precision.HIGHEST)  43.1 us
    dot_general x6, matrix products, newton_step(): jnp.dot(product, piece, precision=lax.Precision.HIGHEST)  32.7 us
    ppermute x1, waiting for transfers between devices, from_behind(): lax.ppermute(value, axis, [(source, source + steps) for source in range(l...  19 us
  transfers between devices with their start and end apart: 8, of which 8 were waited for; matrix products, arithmetic and copies ran while one was open for 14% of the time, Pallas kernels for 0%

commit v1 on v0

--- a/solution.py
+++ b/solution.py
@@ -4,6 +4,28 @@
 from jax.sharding import PartitionSpec as P
 
 ITERS = 3
+
+
+def in_order(blocks, dim):
+    blocks = jnp.moveaxis(blocks, 0, dim)
+    shape = blocks.shape
+    return blocks.reshape(*shape[:dim], shape[dim] * shape[dim + 1], *shape[dim + 2 :])
+
+
+def ring_gather(array, axis, dim):
+    size = lax.axis_size(axis)
+    pairs = [(i, (i + 1) % size) for i in range(size)]
+    back = [(b, a) for a, b in pairs]
+    lower, upper = ([], [])
+    for step in range(size - 1):
+        if step % 2 == 0:
+            lower.append(lax.ppermute(lower[-1] if lower else array, axis, pairs))
+        else:
+            upper.append(lax.ppermute(upper[-1] if upper else array, axis, back))
+    blocks = jnp.stack([*lower[::-1], array, *upper])
+    shift = lax.axis_index(axis) - len(lower)
+    blocks = blocks[(jnp.arange(size) - shift) % size]
+    return in_order(blocks, dim)
 
 
 def from_behind(value, axis, steps):
@@ -24,7 +46,7 @@
     products = tuple(
         (jnp.dot(x, f, precision=lax.Precision.HIGHEST) for x, f in zip(iterates, factors))
     )
-    pieces = jax.tree.map(lambda part: lax.all_gather(part, "dp", axis=0, tiled=True), iterates)
+    pieces = jax.tree.map(lambda part: ring_gather(part, "dp", 0), iterates)
     folded = tuple(
         (
             jnp.dot(product, piece, precision=lax.Precision.HIGHEST)

time: 579 us -> 569 us (0.983)
  the two profiles are of different devices: /device:TPU:1 before, /device:TPU:2 now
where the time goes in v1:
time: 569 us; the launch traced here: 559 us
  waiting for transfers between devices  336 us (59%)
  local copies, waits for them, and re-layouts  87.8 us (15%)
  matrix products  62.3 us (11%)
  starting transfers between devices  53.7 us (9%)
  between operations  18 us (3%)
    ppermute x24, waiting for transfers between devices, ring_gather(): lower.append(lax.ppermute(lower[-1] if lower else array, axis, pairs))  247 us
    psum x1, waiting for transfers between devices, local(): first_sum, second_sum = lax.psum((first_part, second_part), 'dp')  68.1 us
    unnamed x77, local copies, waits for them, and re-layouts  47.5 us
    ppermute x18, starting transfers between devices, ring_gather(): upper.append(lax.ppermute(upper[-1] if upper else array, axis, back))  36.6 us
    dot_general x6, matrix products, newton_step(): jnp.dot(x, f, precision=lax.Precision.HIGHEST)  31.8 us
    gather x6, local copies, waits for them, and re-layouts, ring_gather(): blocks = blocks[(jnp.arange(size) - shift) % size]  30.5 us
    dot_general x6, matrix products, newton_step(): jnp.dot(product, piece, precision=lax.Precision.HIGHEST)  21.7 us
    ppermute x1, waiting for transfers between devices, from_behind(): lax.ppermute(value, axis, [(source, source + steps) for source in range(l...  19.5 us
  transfers between devices with their start and end apart: 44, of which 24 were waited for; matrix products, arithmetic and copies ran while one was open for 21% of the time, Pallas kernels for 0%

profile of v1, /device:TPU:2, one launch (start us, length us, event | category | flops | bytes accessed | tf_op | source)
XLA Modules:
  0.0 559.0 jit_solution(9943215048810233183)
XLA Ops:
  13.9 19.5 %collective-permute-done.21 = bf16[1,1024,1024]{2,1,0:T(8,128)(2,1)S(1)} collective-permute-done((bf16[1,1024,1024]{2,1,0:T(8,128)(2,1)}, bf16[1,1024,1024]{2,1,0:T(8,128)(2,1)S(1)}, u32[]{:S(2)}, u32[]{:S(2)}) %collective-permute-start.21) | collective-permute-done | bytes 2097184 | tf_op jit(solution)/shard_map/ppermute | solution.py:34
  43.1 16.2 %collective-permute-done.22 = f32[128,1024]{1,0:T(8,128)S(1)} collective-permute-done((f32[128,1024]{1,0:T(8,128)S(1)}, f32[128,1024]{1,0:T(8,128)S(1)}, u32[]{:S(2)}, u32[]{:S(2)}) %collective-permute-start.22) | collective-permute-done | bytes 524320 | tf_op jit(solution)/shard_map/ppermute | solution.py:22
  64.2 17.6 %collective-permute-done = f32[128,1024]{1,0:T(8,128)S(1)} collective-permute-done((f32[128,1024]{1,0:T(8,128)S(1)}, f32[128,1024]{1,0:T(8,128)S(1)}, u32[]{:S(2)}, u32[]{:S(2)}) %collective-permute-start) | collective-permute-done | bytes 524320 | tf_op jit(solution)/shard_map/ppermute | solution.py:22
  81.8 22.5 %collective-permute-done.23 = f32[128,1024]{1,0:T(8,128)S(1)} collective-permute-done((f32[128,1024]{1,0:T(8,128)S(1)}, f32[128,1024]{1,0:T(8,128)S(1)}, u32[]{:S(2)}, u32[]{:S(2)}) %collective-permute-start.23) | collective-permute-done | bytes 524320 | tf_op jit(solution)/shard_map/ppermute | solution.py:22
  112.3 14.6 %collective-permute-done.1 = f32[128,1024]{1,0:T(8,128)} collective-permute-done((f32[128,1024]{1,0:T(8,128)S(1)}, f32[128,1024]{1,0:T(8,128)}, u32[]{:S(2)}, u32[]{:S(2)}) %collective-permute-start.1) | collective-permute-done | bytes 524320 | tf_op jit(solution)/shard_map/ppermute | solution.py:22
  127.3 22.0 %collective-permute-done.24 = f32[128,1024]{1,0:T(8,128)} collective-permute-done((f32[128,1024]{1,0:T(8,128)S(1)}, f32[128,1024]{1,0:T(8,128)}, u32[]{:S(2)}, u32[]{:S(2)}) %collective-permute-start.24) | collective-permute-done | bytes 524320 | tf_op jit(solution)/shard_map/ppermute | solution.py:22
  157.2 14.6 %collective-permute-done.2 = f32[128,1024]{1,0:T(8,128)} collective-permute-done((f32[128,1024]{1,0:T(8,128)}, f32[128,1024]{1,0:T(8,128)}, u32[]{:S(2)}, u32[]{:S(2)}) %collective-permute-start.2) | collective-permute-done | bytes 524320 | tf_op jit(solution)/shard_map/ppermute | solution.py:22
  171.8 22.5 %collective-permute-done.25 = f32[128,1024]{1,0:T(8,128)} collective-permute-done((f32[128,1024]{1,0:T(8,128)}, f32[128,1024]{1,0:T(8,128)}, u32[]{:S(2)}, u32[]{:S(2)}) %collective-permute-start.25) | collective-permute-done | bytes 524320 | tf_op jit(solution)/shard_map/ppermute | solution.py:22
  200.8 14.4 %collective-permute-done.3 = f32[128,1024]{1,0:T(8,128)S(1)} collective-permute-done((f32[128,1024]{1,0:T(8,128)}, f32[128,1024]{1,0:T(8,128)S(1)}, u32[]{:S(2)}, u32[]{:S(2)}) %collective-permute-start.3) | collective-permute-done | bytes 524320 | tf_op jit(solution)/shard_map/ppermute | solution.py:22
  225.4 5.4 gather_fusion
  240.6 68.1 %all-reduce.3.cloned.1.call-done = (f32[1024,1024]{1,0:T(8,128)}, f32[1024,1024]{1,0:T(8,128)}) async-done(((f32[1024,1024]{1,0:T(8,128)}, f32[1024,1024]{1,0:T(8,128)}), (f32[1024,1024]{1,0:T(8,128)}, f32[1024,1024]{1,0:T(8,128)})) %all-reduce.3.cloned.1.call-update) | async-done | bytes 8388624 | tf_op jit(solution)/shard_map/psum | solution.py:66
  308.7 9.8 %fusion.2 = f32[1024,128]{1,0:T(8,128)S(1)} fusion(f32[1024,1024]{1,0:T(8,128)} %get-tuple-element.6, f32[]{:T(128)} %bitcast.5, f32[1,2,1,128,1024]{4,3,2,1,0:T(8,128)S(1)} %copy-done.5), kind=kOutput, calls=%fused_computation.11 | convolution fusion | flops 1614807040 | bytes 5242884 | tf_op jit(solution)/shard_map/dot_general | solution.py:47
  321.3 7.5 %fusion.5 = f32[1024,128]{1,0:T(8,128)S(1)} fusion(f32[1024,1024]{1,0:T(8,128)S(1)} %copy-done.14, f32[]{:T(128)} %bitcast.40, f32[1,2,1,128,1024]{4,3,2,1,0:T(8,128)S(1)} %copy-done.5), kind=kOutput, calls=%fused_computation.14 | convolution fusion | flops 1614807040 | bytes 5242884 | tf_op jit(solution)/shard_map/dot_general | solution.py:47
  340.4 8.0 %collective-permute-done.29 = f32[128,1024]{1,0:T(8,128)S(1)} collective-permute-done((f32[128,1024]{1,0:T(8,128)S(1)}, f32[128,1024]{1,0:T(8,128)S(1)}, u32[]{:S(2)}, u32[]{:S(2)}) %collective-permute-start.29) | collective-permute-done | bytes 524320 | tf_op jit(solution)/shard_map/ppermute | solution.py:22
  348.6 11.0 %collective-permute-done.8 = f32[128,1024]{1,0:T(8,128)S(1)} collective-permute-done((f32[128,1024]{1,0:T(8,128)S(1)}, f32[128,1024]{1,0:T(8,128)S(1)}, u32[]{:S(2)}, u32[]{:S(2)}) %collective-permute-start.8) | collective-permute-done | bytes 524320 | tf_op jit(solution)/shard_map/ppermute | solution.py:22
  364.3 6.5 %collective-permute-done.30 = f32[128,1024]{1,0:T(8,128)S(1)} collective-permute-done((f32[128,1024]{1,0:T(8,128)S(1)}, f32[128,1024]{1,0:T(8,128)S(1)}, u32[]{:S(2)}, u32[]{:S(2)}) %collective-permute-start.30) | collective-permute-done | bytes 524320 | tf_op jit(solution)/shard_map/ppermute | solution.py:22
  370.8 11.2 %collective-permute-done.9 = f32[128,1024]{1,0:T(8,128)S(1)} collective-permute-done((f32[128,1024]{1,0:T(8,128)S(1)}, f32[128,1024]{1,0:T(8,128)S(1)}, u32[]{:S(2)}, u32[]{:S(2)}) %collective-permute-start.9) | collective-permute-done | bytes 524320 | tf_op jit(solution)/shard_map/ppermute | solution.py:22
  394.3 10.2 %collective-permute-done.10 = f32[128,1024]{1,0:T(8,128)S(1)} collective-permute-done((f32[128,1024]{1,0:T(8,128)S(1)}, f32[128,1024]{1,0:T(8,128)S(1)}, u32[]{:S(2)}, u32[]{:S(2)}) %collective-permute-start.10) | collective-permute-done | bytes 524320 | tf_op jit(solution)/shard_map/ppermute | solution.py:22
  411.2 5.1 gather_fusion.1
  447.1 10.7 %collective-permute-done.36 = f32[128,1024]{1,0:T(8,128)S(1)} collective-permute-done((f32[128,1024]{1,0:T(8,128)S(1)}, f32[128,1024]{1,0:T(8,128)S(1)}, u32[]{:S(2)}, u32[]{:S(2)}) %collective-permute-start.36) | collective-permute-done | bytes 524320 | tf_op jit(solution)/shard_map/ppermute | solution.py:22
  458.4 10.6 %collective-permute-done.15 = f32[128,1024]{1,0:T(8,128)S(1)} collective-permute-done((f32[128,1024]{1,0:T(8,128)S(1)}, f32[128,1024]{1,0:T(8,128)S(1)}, u32[]{:S(2)}, u32[]{:S(2)}) %collective-permute-start.15) | collective-permute-done | bytes 524320 | tf_op jit(solution)/shard_map/ppermute | solution.py:22
  474.7 5.6 collective-permute-done.37
  480.9 10.6 %collective-permute-done.16 = f32[128,1024]{1,0:T(8,128)S(1)} collective-permute-done((f32[128,1024]{1,0:T(8,128)S(1)}, f32[128,1024]{1,0:T(8,128)S(1)}, u32[]{:S(2)}, u32[]{:S(2)}) %collective-permute-start.16) | collective-permute-done | bytes 524320 | tf_op jit(solution)/shard_map/ppermute | solution.py:22
  505.0 8.9 %collective-permute-done.17 = f32[128,1024]{1,0:T(8,128)S(1)} collective-permute-done((f32[128,1024]{1,0:T(8,128)S(1)}, f32[128,1024]{1,0:T(8,128)S(1)}, u32[]{:S(2)}, u32[]{:S(2)}) %collective-permute-start.17) | collective-permute-done | bytes 524320 | tf_op jit(solution)/shard_map/ppermute | solution.py:22
  (174 shorter events, 187.9 us)
Async XLA Ops:
  6.5 302.2 %all-reduce.3.cloned.1.call-start = ((), (), s32[]{:S(2)}) async-start(), calls=%async_computation | async-start | bytes 16777216 | tf_op jit(solution)/shard_map/psum | solution.py:66
  6.5 26.9 %collective-permute-start.21 = (bf16[1,1024,1024]{2,1,0:T(8,128)(2,1)}, bf16[1,1024,1024]{2,1,0:T(8,128)(2,1)S(1)}, u32[]{:S(2)}, u32[]{:S(2)}) collective-permute-start(bf16[1,1024,1024]{2,1,0:T(8,128)(2,1)} %param.6), channel_id=1, source_target_pairs={{16,0},{32,16},{48,32},{64,48},{80,64},{96,80},{112,96},{128,112},... | collective-permute-start | bytes 6291464 | tf_op jit(solution)/shard_map/ppermute | solution.py:34
  41.2 40.6 %collective-permute-start = (f32[128,1024]{1,0:T(8,128)S(1)}, f32[128,1024]{1,0:T(8,128)S(1)}, u32[]{:S(2)}, u32[]{:S(2)}) collective-permute-start(f32[128,1024]{1,0:T(8,128)S(1)} %get-tuple-element.9), channel_id=1, source_target_pairs={{0,2},{2,4},{4,6},{6,8},{8,10},{10,12},{12,14},{14,0},{1,3},{3,5},... | collective-permute-start | bytes 1572872 | tf_op jit(solution)/shard_map/ppermute | solution.py:22
  59.4 44.9 %collective-permute-start.23 = (f32[128,1024]{1,0:T(8,128)S(1)}, f32[128,1024]{1,0:T(8,128)S(1)}, u32[]{:S(2)}, u32[]{:S(2)}) collective-permute-start(f32[128,1024]{1,0:T(8,128)S(1)} %collective-permute-done.22), channel_id=1, source_target_pairs={{0,2},{2,4},{4,6},{6,8},{8,10},{10,12},{12,14},{14,0},{1,3},{3,5},... | collective-permute-start | bytes 1572872 | tf_op jit(solution)/shard_map/ppermute | solution.py:22
  59.4 44.9 %collective-permute-start.4 = (f32[128,1024]{1,0:T(8,128)S(1)}, f32[128,1024]{1,0:T(8,128)S(1)}, u32[]{:S(2)}, u32[]{:S(2)}) collective-permute-start(f32[128,1024]{1,0:T(8,128)S(1)} %get-tuple-element.9), channel_id=1, source_target_pairs={{2,0},{4,2},{6,4},{8,6},{10,8},{12,10},{14,12},{0,14},{3,1},{5,3},... | collective-permute-start | bytes 1572872 | tf_op jit(solution)/shard_map/ppermute | solution.py:24
  62.6 46.0 %collective-permute-start.26 = (f32[128,1024]{1,0:T(8,128)S(1)}, f32[128,1024]{1,0:T(8,128)S(1)}, u32[]{:S(2)}, u32[]{:S(2)}) collective-permute-start(f32[128,1024]{1,0:T(8,128)S(1)} %get-tuple-element.10), channel_id=1, source_target_pairs={{2,0},{4,2},{6,4},{8,6},{10,8},{12,10},{14,12},{0,14},{3,1},{5,3},... | collective-permute-start | bytes 1572872 | tf_op jit(solution)/shard_map/ppermute | solution.py:24
  81.8 45.0 %collective-permute-start.1 = (f32[128,1024]{1,0:T(8,128)S(1)}, f32[128,1024]{1,0:T(8,128)}, u32[]{:S(2)}, u32[]{:S(2)}) collective-permute-start(f32[128,1024]{1,0:T(8,128)S(1)} %collective-permute-done), channel_id=1, source_target_pairs={{0,2},{2,4},{4,6},{6,8},{8,10},{10,12},{12,14},{14,0},{1,3},{3,5},... | collective-permute-start | bytes 1572872 | tf_op jit(solution)/shard_map/ppermute | solution.py:22
  104.3 45.0 %collective-permute-start.24 = (f32[128,1024]{1,0:T(8,128)S(1)}, f32[128,1024]{1,0:T(8,128)}, u32[]{:S(2)}, u32[]{:S(2)}) collective-permute-start(f32[128,1024]{1,0:T(8,128)S(1)} %collective-permute-done.23), channel_id=1, source_target_pairs={{0,2},{2,4},{4,6},{6,8},{8,10},{10,12},{12,14},{14,0},{1,3},{3,5},... | collective-permute-start | bytes 1572872 | tf_op jit(solution)/shard_map/ppermute | solution.py:22
  104.3 47.7 %collective-permute-start.5 = (f32[128,1024]{1,0:T(8,128)S(1)}, f32[128,1024]{1,0:T(8,128)}, u32[]{:S(2)}, u32[]{:S(2)}) collective-permute-start(f32[128,1024]{1,0:T(8,128)S(1)} %collective-permute-done.4), channel_id=1, source_target_pairs={{2,0},{4,2},{6,4},{8,6},{10,8},{12,10},{14,12},{0,14},{3,1},{5,3},... | collective-permute-start | bytes 1572872 | tf_op jit(solution)/shard_map/ppermute | solution.py:24
  108.6 46.7 %collective-permute-start.27 = (f32[128,1024]{1,0:T(8,128)S(1)}, f32[128,1024]{1,0:T(8,128)}, u32[]{:S(2)}, u32[]{:S(2)}) collective-permute-start(f32[128,1024]{1,0:T(8,128)S(1)} %collective-permute-done.26), channel_id=1, source_target_pairs={{2,0},{4,2},{6,4},{8,6},{10,8},{12,10},{14,12},{0,14},{3,1},{5,3},... | collective-permute-start | bytes 1572872 | tf_op jit(solution)/shard_map/ppermute | solution.py:24
  126.9 44.9 %collective-permute-start.2 = (f32[128,1024]{1,0:T(8,128)}, f32[128,1024]{1,0:T(8,128)}, u32[]{:S(2)}, u32[]{:S(2)}) collective-permute-start(f32[128,1024]{1,0:T(8,128)} %collective-permute-done.1), channel_id=1, source_target_pairs={{0,2},{2,4},{4,6},{6,8},{8,10},{10,12},{12,14},{14,0},{1,3},{3,5},... | collective-permute-start | bytes 1572872 | tf_op jit(solution)/shard_map/ppermute | solution.py:22
  149.3 44.9 %collective-permute-start.25 = (f32[128,1024]{1,0:T(8,128)}, f32[128,1024]{1,0:T(8,128)}, u32[]{:S(2)}, u32[]{:S(2)}) collective-permute-start(f32[128,1024]{1,0:T(8,128)} %collective-permute-done.24), channel_id=1, source_target_pairs={{0,2},{2,4},{4,6},{6,8},{8,10},{10,12},{12,14},{14,0},{1,3},{3,5},... | collective-permute-start | bytes 1572872 | tf_op jit(solution)/shard_map/ppermute | solution.py:22
  152.0 72.5 %collective-permute-start.6 = (f32[128,1024]{1,0:T(8,128)}, f32[128,1024]{1,0:T(8,128)S(1)}, u32[]{:S(2)}, u32[]{:S(2)}) collective-permute-start(f32[128,1024]{1,0:T(8,128)} %collective-permute-done.5), channel_id=1, source_target_pairs={{2,0},{4,2},{6,4},{8,6},{10,8},{12,10},{14,12},{0,14},{3,1},{5,3},... | collective-permute-start | bytes 1572872 | tf_op jit(solution)/shard_map/ppermute | solution.py:24
  155.2 78.4 %collective-permute-start.28 = (f32[128,1024]{1,0:T(8,128)}, f32[128,1024]{1,0:T(8,128)}, u32[]{:S(2)}, u32[]{:S(2)}) collective-permute-start(f32[128,1024]{1,0:T(8,128)} %collective-permute-done.27), channel_id=1, source_target_pairs={{2,0},{4,2},{6,4},{8,6},{10,8},{12,10},{14,12},{0,14},{3,1},{5,3},... | collective-permute-start | bytes 1572872 | tf_op jit(solution)/shard_map/ppermute | solution.py:24
  171.8 43.3 %collective-permute-start.3 = (f32[128,1024]{1,0:T(8,128)}, f32[128,1024]{1,0:T(8,128)S(1)}, u32[]{:S(2)}, u32[]{:S(2)}) collective-permute-start(f32[128,1024]{1,0:T(8,128)} %collective-permute-done.2), channel_id=1, source_target_pairs={{0,2},{2,4},{4,6},{6,8},{8,10},{10,12},{12,14},{14,0},{1,3},{3,5},... | collective-permute-start | bytes 1572872 | tf_op jit(solution)/shard_map/ppermute | solution.py:22
  360.9 27.6 %collective-permute-start.12 = (f32[128,1024]{1,0:T(8,128)S(1)}, f32[128,1024]{1,0:T(8,128)S(1)}, u32[]{:S(2)}, u32[]{:S(2)}) collective-permute-start(f32[128,1024]{1,0:T(8,128)S(1)} %collective-permute-done.11), channel_id=1, source_target_pairs={{2,0},{4,2},{6,4},{8,6},{10,8},{12,10},{14,12},{0,14},{3,1},{5,3},... | collective-permute-start | bytes 1572872 | tf_op jit(solution)/shard_map/ppermute | solution.py:24
  364.2 27.6 %collective-permute-start.34 = (f32[128,1024]{1,0:T(8,128)S(1)}, f32[128,1024]{1,0:T(8,128)}, u32[]{:S(2)}, u32[]{:S(2)}) collective-permute-start(f32[128,1024]{1,0:T(8,128)S(1)} %collective-permute-done.33), channel_id=1, source_target_pairs={{2,0},{4,2},{6,4},{8,6},{10,8},{12,10},{14,12},{0,14},{3,1},{5,3},... | collective-permute-start | bytes 1572872 | tf_op jit(solution)/shard_map/ppermute | solution.py:24
  391.9 38.2 %collective-permute-start.35 = (f32[128,1024]{1,0:T(8,128)}, f32[128,1024]{1,0:T(8,128)}, u32[]{:S(2)}, u32[]{:S(2)}) collective-permute-start(f32[128,1024]{1,0:T(8,128)} %collective-permute-done.34), channel_id=1, source_target_pairs={{2,0},{4,2},{6,4},{8,6},{10,8},{12,10},{14,12},{0,14},{3,1},{5,3},... | collective-permute-start | bytes 1572872 | tf_op jit(solution)/shard_map/ppermute | solution.py:24
  393.4 27.7 %collective-permute-start.32 = (f32[128,1024]{1,0:T(8,128)}, f32[128,1024]{1,0:T(8,128)}, u32[]{:S(2)}, u32[]{:S(2)}) collective-permute-start(f32[128,1024]{1,0:T(8,128)} %collective-permute-done.31), channel_id=1, source_target_pairs={{0,2},{2,4},{4,6},{6,8},{8,10},{10,12},{12,14},{14,0},{1,3},{3,5},... | collective-permute-start | bytes 1572872 | tf_op jit(solution)/shard_map/ppermute | solution.py:22
  446.9 26.8 %collective-permute-start.40 = (f32[128,1024]{1,0:T(8,128)S(1)}, f32[128,1024]{1,0:T(8,128)S(1)}, u32[]{:S(2)}, u32[]{:S(2)}) collective-permute-start(f32[128,1024]{1,0:T(8,128)S(1)} %fusion.30), channel_id=1, source_target_pairs={{2,0},{4,2},{6,4},{8,6},{10,8},{12,10},{14,12},{0,14},{3,1},{5,3},... | collective-permute-start | bytes 1572872 | tf_op jit(solution)/shard_map/ppermute | solution.py:24
  471.0 29.2 %collective-permute-start.19 = (f32[128,1024]{1,0:T(8,128)S(1)}, f32[128,1024]{1,0:T(8,128)S(1)}, u32[]{:S(2)}, u32[]{:S(2)}) collective-permute-start(f32[128,1024]{1,0:T(8,128)S(1)} %collective-permute-done.18), channel_id=1, source_target_pairs={{2,0},{4,2},{6,4},{8,6},{10,8},{12,10},{14,12},{0,14},{3,1},{5,3},... | collective-permute-start | bytes 1572872 | tf_op jit(solution)/shard_map/ppermute | solution.py:24
  473.7 29.2 %collective-permute-start.41 = (f32[128,1024]{1,0:T(8,128)S(1)}, f32[128,1024]{1,0:T(8,128)}, u32[]{:S(2)}, u32[]{:S(2)}) collective-permute-start(f32[128,1024]{1,0:T(8,128)S(1)} %collective-permute-done.40), channel_id=1, source_target_pairs={{2,0},{4,2},{6,4},{8,6},{10,8},{12,10},{14,12},{0,14},{3,1},{5,3},... | collective-permute-start | bytes 1572872 | tf_op jit(solution)/shard_map/ppermute | solution.py:24
  500.2 27.7 %collective-permute-start.20 = (f32[128,1024]{1,0:T(8,128)S(1)}, f32[128,1024]{1,0:T(8,128)S(1)}, u32[]{:S(2)}, u32[]{:S(2)}) collective-permute-start(f32[128,1024]{1,0:T(8,128)S(1)} %collective-permute-done.19), channel_id=1, source_target_pairs={{2,0},{4,2},{6,4},{8,6},{10,8},{12,10},{14,12},{0,14},{3,1},{5,3},... | collective-permute-start | bytes 1572872 | tf_op jit(solution)/shard_map/ppermute | solution.py:24
  502.8 33.7 %collective-permute-start.42 = (f32[128,1024]{1,0:T(8,128)}, f32[128,1024]{1,0:T(8,128)}, u32[]{:S(2)}, u32[]{:S(2)}) collective-permute-start(f32[128,1024]{1,0:T(8,128)} %collective-permute-done.41), channel_id=1, source_target_pairs={{2,0},{4,2},{6,4},{8,6},{10,8},{12,10},{14,12},{0,14},{3,1},{5,3},... | collective-permute-start | bytes 1572872 | tf_op jit(solution)/shard_map/ppermute | solution.py:24
  (38 other events, 949.9 us)
Sparse Core Ops, SparseCore 0:
  38.1 270.6 all-reduce.2
